TPU v7x, 32 devices: a whole 2x2x4 slice. The times are simulated.
32 devices in a mesh: expert: 4 (over y, x), dp: 8 (over z, core).
Axes of the slice: x: 2, y: 2, z: 4, core: 2. Of those that a mesh axis runs over, the one named last changes fastest.
Arguments:
- tokens: bfloat16 [1024, 5120], P('dp', 'expert'), may hold values from -6 to 6
- routes: int32 [1024, 2], P('dp'), may hold values from 0 to 7, all different within a row; in each aligned block of 128 rows (0 to 127, 128 to 255, ...) at most 48 rows name the same one
- combine: bfloat16 [1024, 2], P('dp'), may hold values from 0.099609375 to 1
- cotangent: bfloat16 [1024, 5120], P('dp', 'expert'), may hold values from -1.5 to 1.5
- w_gate: bfloat16 [8, 5120, 768], P('dp', 'expert'), may hold values from -0.078125 to 0.078125
- w_up: bfloat16 [8, 5120, 768], P('dp', 'expert'), may hold values from -0.078125 to 0.078125
- w_down: bfloat16 [8, 768, 5120], P('dp', None, 'expert'), may hold values from -0.21875 to 0.21875
Outputs:
- token_grad: bfloat16 [1024, 5120], P('dp', 'expert')
- combine_grad: float32 [1024, 2], P('dp')
- grad_gate: bfloat16 [8, 5120, 768], P('dp', 'expert')
- grad_up: bfloat16 [8, 5120, 768], P('dp', 'expert')
- grad_down: bfloat16 [8, 768, 5120], P('dp', None, 'expert')
Inputs may be any that keep to these rules, and one draw needn't show every extreme that they name: `routes`: each token names 2 different experts. The tokens of one group name any one expert at most 48 times, a bound that some block reaches.
All inputs are finite; a program needn't handle non-finite values.
Results may differ from a plain program's by a relative error of at most 0.018.
Values may be sent and summed in bfloat16 or wider, within the bound.
No kernel may reach another device: no remote copies, remote signals or barrier semaphores. Data moves between devices by JAX's collectives and lax.ppermute only.
A program may use at most 64 MiB of HBM per device.

v0:
```python
import jax
import jax.numpy as jnp
from jax import lax
from jax.sharding import PartitionSpec as P


def contract_last(matrix_a, matrix_b):
    return lax.dot_general(
        matrix_a, matrix_b, (((1,), (1,)), ((), ())), preferred_element_type=jnp.float32
    )


def contract_first(matrix_a, matrix_b):
    return lax.dot_general(
        matrix_a, matrix_b, (((0,), (0,)), ((), ())), preferred_element_type=jnp.float32
    )


def swiglu_grads(pre_gate, pre_up, back_hidden, weights):
    sigmas = jax.nn.sigmoid(pre_gate)
    active = pre_gate * sigmas
    hidden = (active * pre_up).astype(jnp.bfloat16)
    scaled = weights[:, None] * back_hidden
    grad_gate_pre = (scaled * pre_up * sigmas * (1.0 + pre_gate * (1.0 - sigmas))).astype(
        jnp.bfloat16
    )
    grad_up_pre = (scaled * active).astype(jnp.bfloat16)
    return (hidden, grad_gate_pre, grad_up_pre)


def body(tokens, routes, combine, cotangent, w_gate, w_up, w_down):
    tok_rows, slice_width = tokens.shape
    top_routes = routes.shape[1]
    experts = lax.axis_size("dp")
    capacity = 3 * tok_rows * top_routes // (2 * experts)
    route_count = tok_rows * top_routes
    slot_total = experts * capacity
    route_flat = routes.reshape(route_count)
    onehot = (route_flat[:, None] == jnp.arange(experts, dtype=jnp.int32)[None, :]).astype(
        jnp.int32
    )
    slot_rank = jnp.sum((jnp.cumsum(onehot, axis=0) - onehot) * onehot, axis=1)
    places = route_flat * capacity + slot_rank
    source = jnp.full((slot_total,), route_count, jnp.int32)
    source = source.at[places].set(jnp.arange(route_count, dtype=jnp.int32))
    blank_row = jnp.zeros((1, slice_width), jnp.bfloat16)
    token_send = jnp.concatenate([tokens, blank_row], axis=0)[source // top_routes]
    cot_send = jnp.concatenate([cotangent, blank_row], axis=0)[source // top_routes]
    comb_send = jnp.concatenate(
        [combine.reshape(route_count), jnp.zeros((1,), jnp.bfloat16)], axis=0
    )[source]
    arrived_tok, arrived_cot, arrived_comb = (
        lax.all_to_all(
            token_send.reshape(experts, capacity, slice_width),
            "dp",
            split_axis=0,
            concat_axis=0,
            tiled=True,
        ),
        lax.all_to_all(
            cot_send.reshape(experts, capacity, slice_width),
            "dp",
            split_axis=0,
            concat_axis=0,
            tiled=True,
        ),
        lax.all_to_all(
            comb_send.reshape(experts, capacity), "dp", split_axis=0, concat_axis=0, tiled=True
        ),
    )
    token_slots = arrived_tok.reshape(slot_total, slice_width)
    cot_slots = arrived_cot.reshape(slot_total, slice_width)
    comb_slots = arrived_comb.reshape(slot_total).astype(jnp.float32)
    gate_mat = w_gate[0]
    up_mat = w_up[0]
    down_mat = w_down[0]
    partials = jnp.stack(
        [
            jnp.dot(token_slots, gate_mat, preferred_element_type=jnp.float32),
            jnp.dot(token_slots, up_mat, preferred_element_type=jnp.float32),
            contract_last(cot_slots, down_mat),
        ],
        axis=1,
    )
    summed = lax.psum_scatter(
        partials.astype(jnp.bfloat16), "expert", scatter_dimension=2, tiled=True
    ).astype(jnp.float32)
    hidden_part, gate_part, up_part = swiglu_grads(
        summed[:, 0], summed[:, 1], summed[:, 2], comb_slots
    )
    slot_comb = jnp.sum(hidden_part.astype(jnp.float32) * summed[:, 2], axis=1)
    joined = lax.all_gather(
        jnp.stack([hidden_part, gate_part, up_part], axis=1), "expert", axis=2, tiled=True
    )
    hidden = joined[:, 0]
    grad_gate_pre = joined[:, 1]
    grad_up_pre = joined[:, 2]
    slot_dx = contract_last(grad_gate_pre, gate_mat) + contract_last(grad_up_pre, up_mat)
    scaled_dy = (comb_slots[:, None] * cot_slots.astype(jnp.float32)).astype(jnp.bfloat16)
    grad_gate = contract_first(token_slots, grad_gate_pre).astype(jnp.bfloat16)[None]
    grad_up = contract_first(token_slots, grad_up_pre).astype(jnp.bfloat16)[None]
    grad_down = contract_first(hidden, scaled_dy).astype(jnp.bfloat16)[None]
    back_dx, back_comb = (
        lax.all_to_all(
            slot_dx.reshape(experts, capacity, slice_width).astype(jnp.bfloat16),
            "dp",
            split_axis=0,
            concat_axis=0,
            tiled=True,
        ).astype(jnp.float32),
        lax.all_to_all(
            slot_comb.reshape(experts, capacity).astype(jnp.bfloat16),
            "dp",
            split_axis=0,
            concat_axis=0,
            tiled=True,
        ).astype(jnp.float32),
    )
    route_dx = back_dx.reshape(slot_total, slice_width)[places].reshape(
        tok_rows, top_routes, slice_width
    )
    token_grad = jnp.sum(route_dx, axis=1).astype(jnp.bfloat16)
    comb_part = back_comb.reshape(slot_total)[places].reshape(tok_rows, top_routes)
    combine_grad = lax.psum(comb_part, "expert")
    return (token_grad, combine_grad, grad_gate, grad_up, grad_down)


def solution(mesh):
    in_specs = (
        P("dp", "expert"),
        P("dp", None),
        P("dp", None),
        P("dp", "expert"),
        P("dp", "expert", None),
        P("dp", "expert", None),
        P("dp", None, "expert"),
    )
    out_specs = (
        P("dp", "expert"),
        P("dp", None),
        P("dp", "expert", None),
        P("dp", "expert", None),
        P("dp", None, "expert"),
    )
    return jax.shard_map(body, mesh=mesh, in_specs=in_specs, out_specs=out_specs, check_vma=False)
```

profile of v0, /device:TPU:0, one launch (start us, length us, event | category | flops | bytes accessed | tf_op | source)
XLA Modules:
  0.0 218.3 jit_solution(15409593457587932573)
XLA Ops:
  7.2 0.8 broadcast_multiply_fusion
  8.0 0.8 copy.25
  9.3 0.6 reduce-window.6
  9.9 0.2 slice_reduce_fusion
  10.3 1.4 scatter_custom_fusion
  11.7 1.0 concatenate.9
  12.7 2.8 %gather_fusion = bf16[384,1280]{1,0:T(8,128)(2,1)} fusion(bf16[129,1280]{1,0:T(8,128)(2,1)S(1)} %concatenate.9, s32[1024]{0:T(1024)S(1)} %get-tuple-element.26), kind=kCustom, calls=%fused_computation | custom fusion | bytes 1967616 | tf_op jit(solution)/shard_map/gather | solution.py:47
  15.5 6.3 %all-to-all-start = ((bf16[8,48,1280]{2,1,0:T(8,128)(2,1)}), bf16[8,48,1280]{2,1,0:T(8,128)(2,1)S(1)}, u32[]{:S(2)}, u32[]{:S(2)}) async-start(bf16[8,48,1280]{2,1,0:T(8,128)(2,1)} %bitcast.4), calls=%async_computation | async-start | bytes 1966080 | tf_op jit(solution)/shard_map/all_to_all | solution.py:53
  21.8 1.0 concatenate.10
  22.8 2.8 %gather_fusion.1 = bf16[384,1280]{1,0:T(8,128)(2,1)} fusion(bf16[129,1280]{1,0:T(8,128)(2,1)S(1)} %concatenate.10, s32[1024]{0:T(1024)S(1)} %get-tuple-element.26), kind=kCustom, calls=%fused_computation.1 | custom fusion | bytes 1967616 | tf_op jit(solution)/shard_map/gather | solution.py:48
  25.6 21.4 %all-to-all-done = bf16[8,48,1280]{2,1,0:T(8,128)(2,1)S(1)} async-done(((bf16[8,48,1280]{2,1,0:T(8,128)(2,1)}), bf16[8,48,1280]{2,1,0:T(8,128)(2,1)S(1)}, u32[]{:S(2)}, u32[]{:S(2)}) %all-to-all-start) | async-done | bytes 983072 | tf_op jit(solution)/shard_map/all_to_all | solution.py:53
  47.0 0.9 copy-done.3
  48.0 3.6 %all-to-all-start.1 = ((bf16[8,48,1280]{2,1,0:T(8,128)(2,1)}), bf16[8,48,1280]{2,1,0:T(8,128)(2,1)S(1)}, u32[]{:S(2)}, u32[]{:S(2)}) async-start(bf16[8,48,1280]{2,1,0:T(8,128)(2,1)} %bitcast.107), calls=%async_computation.1 | async-start | bytes 1966080 | tf_op jit(solution)/shard_map/all_to_all | solution.py:60
  51.6 2.9 %fusion.25 = bf16[384,1,768]{2,0,1:T(8,128)(2,1)S(1)} fusion(bf16[384,1280]{1,0:T(8,128)(2,1)} %bitcast.109, bf16[1,1280,768]{2,1,0:T(8,128)(2,1)} %param.12), kind=kOutput, calls=%fused_computation.29 | convolution fusion | flops 755269632 | bytes 3538944 | tf_op jit(solution)/shard_map/dot_general | solution.py:80
  54.5 1.7 fusion.28
  56.2 20.4 %all-to-all-done.1 = bf16[8,48,1280]{2,1,0:T(8,128)(2,1)S(1)} async-done(((bf16[8,48,1280]{2,1,0:T(8,128)(2,1)}), bf16[8,48,1280]{2,1,0:T(8,128)(2,1)S(1)}, u32[]{:S(2)}, u32[]{:S(2)}) %all-to-all-start.1) | async-done | bytes 983072 | tf_op jit(solution)/shard_map/all_to_all | solution.py:60
  76.6 2.9 %fusion.22 = bf16[384,1,768]{2,0,1:T(8,128)(2,1)S(1)} fusion(bf16[384,1280]{1,0:T(8,128)(2,1)S(1)} %bitcast.106, bf16[1,768,1280]{2,1,0:T(8,128)(2,1)} %param.13), kind=kOutput, calls=%fused_computation.28 | convolution fusion | flops 755269632 | bytes 3538944 | tf_op jit(solution)/shard_map/dot_general | solution.py:8
  79.5 1.4 pad_maximum_fusion
  81.0 5.2 %copy.32 = bf16[384,3,768]{0,1,2:T(4,128)(2,1)} copy(bf16[384,3,768]{2,0,1:T(8,128)(2,1)} %pad_maximum_fusion) | data formatting | bytes 3538944
  86.2 3.2 %copy.34 = bf16[96,8,3,384]{3,1,2,0:T(8,128)(2,1)} copy(bf16[96,8,3,384]{3,2,1,0:T(4,128)(2,1)} %bitcast.104) | data formatting | bytes 3538944
  89.6 0.1 reshape.142
  89.7 2.8 %gather_fusion.2 = bf16[384]{0:T(512)(128)(2,1)S(1)} fusion(bf16[257]{0:T(512)(128)(2,1)S(1)} %pad_maximum_fusion.2, s32[1024]{0:T(1024)S(1)} %get-tuple-element.25), kind=kCustom, calls=%fused_computation.2 | custom fusion | bytes 3072 | tf_op jit(solution)/shard_map/gather | solution.py:49
  92.6 7.9 %all_to_all.31 = bf16[8,1,48]{2,1,0:T(2,128)(2,1)S(1)} all-to-all(bf16[8,1,48]{2,1,0:T(2,128)(2,1)S(1)} %all_to_all.25), channel_id=1, replica_groups=mesh['expert'=4,'dp'=8] {'dp'}, dimensions={0} | all-to-all | bytes 1536 | tf_op jit(solution)/shard_map/all_to_all | solution.py:67
  100.6 20.2 %reduce-scatter.4.cloned.1.call-done = bf16[192,1152]{1,0:T(8,128)(2,1)} async-done(((bf16[768,1152]{1,0:T(8,128)(2,1)}), bf16[192,1152]{1,0:T(8,128)(2,1)}) %reduce-scatter.4.cloned.1.call-update) | async-done | bytes 442384
  120.9 1.4 reshape.204
  122.3 1.3 copy.33
  123.6 1.2 convert_element_type.95
  124.8 0.2 multiply_convert_fusion.2
  125.0 1.0 pad_maximum_fusion.1
  126.0 2.1 copy.29
  128.1 0.2 fusion.31
  128.3 0.7 convert_element_type.121
  129.0 4.6 %all-to-all-start.4 = ((bf16[8,1,48]{2,1,0:T(2,128)(2,1)}), bf16[8,1,48]{2,1,0:T(2,128)(2,1)S(1)}, u32[]{:S(2)}, u32[]{:S(2)}) async-start(bf16[8,1,48]{2,1,0:T(2,128)(2,1)} %convert_element_type.121), calls=%async_computation.4 | async-start | bytes 8192 | tf_op jit(solution)/shard_map/all_to_all | solution.py:111
  133.6 27.2 %all-gather.2.cloned.1.call-done = bf16[384,3,768]{0,2,1:T(8,128)(2,1)} async-done(((bf16[384,3,192]{0,2,1:T(8,128)(2,1)}), bf16[384,3,768]{0,2,1:T(8,128)(2,1)}) %all-gather.2.cloned.1.call-update) | async-done | bytes 1769488 | tf_op jit(solution)/shard_map/all_gather | solution.py:92
  160.8 2.2 %fusion.9 = f32[384,1280]{1,0:T(8,128)S(1)} fusion(bf16[1,1280,768]{2,1,0:T(8,128)(2,1)S(1)} %copy-done, bf16[384,3,768]{0,2,1:T(8,128)(2,1)} %all-gather.2.cloned.1.call-done), kind=kOutput, calls=%fused_computation.19 | convolution fusion | flops 754974720 | bytes 4521984 | tf_op jit(solution)/shard_map/dot_general | solution.py:8
  163.0 3.1 %fusion.3 = bf16[384,1280]{1,0:T(8,128)(2,1)} fusion(f32[384,1280]{1,0:T(8,128)S(1)} %fusion.9, bf16[1,1280,768]{2,1,0:T(8,128)(2,1)S(1)} %copy-done.9, bf16[384,3,768]{0,2,1:T(8,128)(2,1)} %all-gather.2.cloned.1.call-done), kind=kOutput, calls=%fused_computation.13 | convolution fusion | flops 755957760 | bytes 5505024 | tf_op jit(solution)/shard_map/dot_general | solution.py:8
  166.1 4.7 %all-to-all-start.3 = ((bf16[8,48,1280]{2,1,0:T(8,128)(2,1)}), bf16[8,48,1280]{2,1,0:T(8,128)(2,1)}, u32[]{:S(2)}, u32[]{:S(2)}) async-start(bf16[8,48,1280]{2,1,0:T(8,128)(2,1)} %bitcast.113), calls=%async_computation.3 | async-start | bytes 1966080 | tf_op jit(solution)/shard_map/all_to_all | solution.py:104
  170.9 1.2 multiply_convert_fusion
  172.1 1.9 gather_fusion.4
  174.2 16.2 %psum.7 = f32[128,2]{1,0:T(8,128)S(1)} all-reduce(f32[128,2]{1,0:T(8,128)S(1)} %reshape.146), channel_id=1, replica_groups=mesh['expert'=4,'dp'=8] {'expert'}, use_global_device_ids=true, to_apply=%region_7.8 | all-reduce | flops 256 | bytes 2048 | tf_op jit(solution)/shard_map/psum | solution.py:124
  190.4 0.6 copy.31
  191.0 4.0 %fusion = bf16[1,1280,768]{2,1,0:T(8,128)(2,1)} fusion(bf16[384,1280]{1,0:T(8,128)(2,1)} %bitcast.110, bf16[384,3,768]{0,2,1:T(8,128)(2,1)} %all-gather.2.cloned.1.call-done), kind=kOutput, calls=%fused_computation.10 | convolution fusion | flops 755957760 | bytes 3538944 | tf_op jit(solution)/shard_map/dot_general | solution.py:14
  195.0 2.5 %fusion.1 = bf16[1,1280,768]{2,1,0:T(8,128)(2,1)} fusion(bf16[384,1280]{1,0:T(8,128)(2,1)S(1)} %bitcast.112, bf16[384,3,768]{0,2,1:T(8,128)(2,1)S(1)} %copy-done.10), kind=kOutput, calls=%fused_computation.11 | convolution fusion | flops 755957760 | bytes 3538944 | tf_op jit(solution)/shard_map/dot_general | solution.py:14
  197.6 2.4 %fusion.2 = bf16[1,768,1280]{2,1,0:T(8,128)(2,1)} fusion(bf16[384,1280]{1,0:T(8,128)(2,1)S(1)} %bitcast.114, bf16[384,3,768]{0,2,1:T(8,128)(2,1)S(1)} %copy-done.10), kind=kOutput, calls=%fused_computation.12 | convolution fusion | flops 755957760 | bytes 3538944 | tf_op jit(solution)/shard_map/dot_general | solution.py:14
  200.0 2.6 %bitcast_convert_fusion = f32[384,1280]{1,0:T(8,128)} fusion(bf16[8,48,1280]{2,1,0:T(8,128)(2,1)} %all-to-all-done.3), kind=kLoop, calls=%fused_computation.31 | loop fusion | flops 491520 | bytes 2949120 | tf_op jit(solution)/shard_map/reshape | solution.py:119
  202.6 3.3 %gather_fusion.3 = f32[256,1280]{1,0:T(8,128)S(1)} fusion(f32[384,1280]{1,0:T(8,128)} %bitcast_convert_fusion, s32[1024]{0:T(1024)S(1)} %pad_clamp_fusion), kind=kCustom, calls=%fused_computation.3 | custom fusion | bytes 2622464 | tf_op jit(solution)/shard_map/gather | solution.py:119
  206.0 1.8 reshape.145
  207.8 3.6 %reduce_sum.31 = bf16[128,1280]{1,0:T(8,128)(2,1)} reduce(f32[128,2,1280]{2,1,0:T(2,128)} %reshape.145, f32[]{:T(128)} %constant.40.clone.1), dimensions={1}, to_apply=%region_5.6 | reduce | flops 163840 | bytes 1638404 | tf_op jit(solution)/shard_map/reduce_sum | solution.py:122
  (49 shorter events, 1.4 us)
Async XLA Ops:
  7.2 47.3 %copy-start = (bf16[1,1280,768]{2,1,0:T(8,128)(2,1)S(1)}, bf16[1,1280,768]{2,1,0:T(8,128)(2,1)}, u32[]{:S(2)}) copy-start(bf16[1,1280,768]{2,1,0:T(8,128)(2,1)} %param.11) | copy-start | bytes 5898244
  15.5 31.5 %all-to-all-start = ((bf16[8,48,1280]{2,1,0:T(8,128)(2,1)}), bf16[8,48,1280]{2,1,0:T(8,128)(2,1)S(1)}, u32[]{:S(2)}, u32[]{:S(2)}) async-start(bf16[8,48,1280]{2,1,0:T(8,128)(2,1)} %bitcast.4), calls=%async_computation | async-start | bytes 1966080 | tf_op jit(solution)/shard_map/all_to_all | solution.py:53
  47.0 0.9 copy-start.3
  48.0 28.7 %all-to-all-start.1 = ((bf16[8,48,1280]{2,1,0:T(8,128)(2,1)}), bf16[8,48,1280]{2,1,0:T(8,128)(2,1)S(1)}, u32[]{:S(2)}, u32[]{:S(2)}) async-start(bf16[8,48,1280]{2,1,0:T(8,128)(2,1)} %bitcast.107), calls=%async_computation.1 | async-start | bytes 1966080 | tf_op jit(solution)/shard_map/all_to_all | solution.py:60
  51.5 69.4 %reduce-scatter.4.cloned.1.call-start = ((), (), s32[]{:S(2)}) async-start(), calls=%async_computation.7 | async-start | bytes 2211840
  51.6 2.9 %copy-start.4 = (bf16[8,48,1280]{2,1,0:T(8,128)(2,1)S(1)}, bf16[8,48,1280]{2,1,0:T(8,128)(2,1)}, u32[]{:S(2)}) copy-start(bf16[8,48,1280]{2,1,0:T(8,128)(2,1)} %copy-done.3) | copy-start | bytes 2949124
  76.6 2.9 %copy-start.1 = (bf16[8,48,1280]{2,1,0:T(8,128)(2,1)}, bf16[8,48,1280]{2,1,0:T(8,128)(2,1)S(1)}, u32[]{:S(2)}) copy-start(bf16[8,48,1280]{2,1,0:T(8,128)(2,1)S(1)} %all-to-all-done.1) | copy-start | bytes 2949124
  76.6 2.9 %copy-start.7 = (bf16[384,1,768]{2,0,1:T(8,128)(2,1)S(1)}, bf16[384,1,768]{2,0,1:T(8,128)(2,1)}, u32[]{:S(2)}) copy-start(bf16[384,1,768]{2,0,1:T(8,128)(2,1)} %fusion.28) | copy-start | bytes 1769476
  86.1 3.3 %copy-start.8 = (bf16[128,2]{0,1:T(2,128)(2,1)S(1)}, bf16[128,2]{0,1:T(2,128)(2,1)}, u32[]{:S(2)}) copy-start(bf16[128,2]{0,1:T(2,128)(2,1)} %param.9) | copy-start | bytes 1540
  89.4 71.4 %all-gather.2.cloned.1.call-start = ((), (), s32[]{:S(2)}) async-start(), calls=%async_computation.6 | async-start | bytes 2211840 | tf_op jit(solution)/shard_map/all_gather | solution.py:92
  129.0 37.1 %all-to-all-start.4 = ((bf16[8,1,48]{2,1,0:T(2,128)(2,1)}), bf16[8,1,48]{2,1,0:T(2,128)(2,1)S(1)}, u32[]{:S(2)}, u32[]{:S(2)}) async-start(bf16[8,1,48]{2,1,0:T(2,128)(2,1)} %convert_element_type.121), calls=%async_computation.4 | async-start | bytes 8192 | tf_op jit(solution)/shard_map/all_to_all | solution.py:111
  160.8 2.2 %copy-start.9 = (bf16[1,1280,768]{2,1,0:T(8,128)(2,1)S(1)}, bf16[1,1280,768]{2,1,0:T(8,128)(2,1)}, u32[]{:S(2)}) copy-start(bf16[1,1280,768]{2,1,0:T(8,128)(2,1)} %param.12) | copy-start | bytes 5898244
  166.1 4.8 %copy-start.2 = (bf16[8,48,1280]{2,1,0:T(8,128)(2,1)S(1)}, bf16[8,48,1280]{2,1,0:T(8,128)(2,1)}, u32[]{:S(2)}) copy-start(bf16[8,48,1280]{2,1,0:T(8,128)(2,1)} %copy-done.1) | copy-start | bytes 2949124
  166.1 33.9 %all-to-all-start.3 = ((bf16[8,48,1280]{2,1,0:T(8,128)(2,1)}), bf16[8,48,1280]{2,1,0:T(8,128)(2,1)}, u32[]{:S(2)}, u32[]{:S(2)}) async-start(bf16[8,48,1280]{2,1,0:T(8,128)(2,1)} %bitcast.113), calls=%async_computation.3 | async-start | bytes 1966080 | tf_op jit(solution)/shard_map/all_to_all | solution.py:104
  174.2 20.8 %copy-start.5 = (bf16[8,48,1280]{2,1,0:T(8,128)(2,1)S(1)}, bf16[8,48,1280]{2,1,0:T(8,128)(2,1)}, u32[]{:S(2)}) copy-start(bf16[8,48,1280]{2,1,0:T(8,128)(2,1)} %copy-done.3) | copy-start | bytes 2949124
  191.0 4.0 %copy-start.10 = (bf16[384,3,768]{0,2,1:T(8,128)(2,1)S(1)}, bf16[384,3,768]{0,2,1:T(8,128)(2,1)}, u32[]{:S(2)}) copy-start(bf16[384,3,768]{0,2,1:T(8,128)(2,1)} %all-gather.2.cloned.1.call-done) | copy-start | bytes 5308420
  195.0 2.5 %copy-start.6 = (bf16[8,48,1280]{2,1,0:T(8,128)(2,1)S(1)}, bf16[8,48,1280]{2,1,0:T(8,128)(2,1)}, u32[]{:S(2)}) copy-start(bf16[8,48,1280]{2,1,0:T(8,128)(2,1)} %multiply_convert_fusion) | copy-start | bytes 2949124
Sparse Core Ops, SparseCore 0:
  89.5 31.3 reduce-scatter.3
  128.2 32.5 all-gather.1
where the time goes:
time: 219 us; the launch traced here: 218 us
  waiting for transfers between devices  89.4 us (41%)
  local copies, waits for them, and re-layouts  36.5 us (17%)
  blocking collectives  24.1 us (11%)
  matrix products  21.7 us (10%)
  starting transfers between devices  19.3 us (9%)
  between operations  14.3 us (7%)
  other arithmetic  13 us (6%)
    all_gather x1, waiting for transfers between devices, body(): lax.all_gather(jnp.stack([hidden_part, gate_part, up_part], axis=1), 'exp...  27.2 us
    all_to_all x1, waiting for transfers between devices, body(): lax.all_to_all(token_send.reshape(experts, capacity, slice_width), 'dp',...  21.4 us
    all_to_all x1, waiting for transfers between devices, body(): lax.all_to_all(cot_send.reshape(experts, capacity, slice_width), 'dp', sp...  20.4 us
    unnamed x3, waiting for transfers between devices  20.3 us
    psum x1, blocking collectives, body(): combine_grad = lax.psum(comb_part, 'expert')  16.2 us
    unnamed x29, local copies, waits for them, and re-layouts  13.6 us
    dot_general x3, matrix products, contract_first(): lax.dot_general(matrix_a, matrix_b, (((0,), (0,)), ((), ())), preferred_e...  8.94 us
    dot_general x3, matrix products, contract_last(): lax.dot_general(matrix_a, matrix_b, (((1,), (1,)), ((), ())), preferred_e...  8.15 us
  transfers between devices with their start and end apart: 6, of which 4 were waited for; matrix products, arithmetic and copies ran while one was open for 14% of the time, Pallas kernels for 0%

commit v1 on v0

--- a/solution.py
+++ b/solution.py
@@ -121,7 +121,11 @@
     )
     token_grad = jnp.sum(route_dx, axis=1).astype(jnp.bfloat16)
     comb_part = back_comb.reshape(slot_total)[places].reshape(tok_rows, top_routes)
-    combine_grad = lax.psum(comb_part, "expert")
+    combine_grad = comb_part
+    for hop in (1, 2):
+        combine_grad = combine_grad + lax.ppermute(
+            combine_grad, "expert", [(dev, dev ^ hop) for dev in range(4)]
+        )
     return (token_grad, combine_grad, grad_gate, grad_up, grad_down)
 
 

time: 219 us -> 215 us (0.982)
  blocking collectives: 24.1 us -> 7.92 us
  waiting for transfers between devices: 89.4 us -> 98.6 us
  starting transfers between devices: 19.3 us -> 22.4 us
    psum x1 -> x0, blocking collectives: 16.2 us -> none  [body(): combine_grad = lax.psum(comb_part, 'expert')]
    ppermute x0 -> x2, waiting for transfers between devices: none -> 4.66 us  [body(): lax.ppermute(combine_grad, 'expert', [(dev, dev ^ hop) for dev in range(4)])]
    all_to_all x1, waiting for transfers between devices: 0.01 us -> 4.57 us  [body(): lax.all_to_all(slot_dx.reshape(experts, capacity, slice_width).astype(jnp...]
    ppermute x0 -> x2, starting transfers between devices: none -> 3.06 us  [body(): lax.ppermute(combine_grad, 'expert', [(dev, dev ^ hop) for dev in range(4)])]
  transfers between devices with their start and end apart: 6 -> 8, of which waited for: 4 -> 7; matrix products, arithmetic and copies ran while one was open for 14% -> 14% of each run, Pallas kernels for 0% -> 0%
where the time goes in v1:
time: 215 us; the launch traced here: 214 us
  waiting for transfers between devices  98.6 us (46%)
  local copies, waits for them, and re-layouts  36.6 us (17%)
  starting transfers between devices  22.4 us (10%)
  matrix products  21.7 us (10%)
  between operations  14.3 us (7%)
  other arithmetic  12.9 us (6%)
  blocking collectives  7.92 us (4%)
    all_gather x1, waiting for transfers between devices, body(): lax.all_gather(jnp.stack([hidden_part, gate_part, up_part], axis=1), 'exp...  27.2 us
    all_to_all x1, waiting for transfers between devices, body(): lax.all_to_all(token_send.reshape(experts, capacity, slice_width), 'dp',...  21.4 us
    all_to_all x1, waiting for transfers between devices, body(): lax.all_to_all(cot_send.reshape(experts, capacity, slice_width), 'dp', sp...  20.4 us
    unnamed x3, waiting for transfers between devices  20.3 us
    unnamed x29, local copies, waits for them, and re-layouts  13.8 us
    dot_general x3, matrix products, contract_first(): lax.dot_general(matrix_a, matrix_b, (((0,), (0,)), ((), ())), preferred_e...  8.94 us
    dot_general x3, matrix products, contract_last(): lax.dot_general(matrix_a, matrix_b, (((1,), (1,)), ((), ())), preferred_e...  8.15 us
    all_to_all x1, blocking collectives, body(): lax.all_to_all(comb_send.reshape(experts, capacity), 'dp', split_axis=0,...  7.92 us
  transfers between devices with their start and end apart: 8, of which 7 were waited for; matrix products, arithmetic and copies ran while one was open for 14% of the time, Pallas kernels for 0%

profile of v1, /device:TPU:0, one launch (start us, length us, event | category | flops | bytes accessed | tf_op | source)
XLA Modules:
  0.0 214.4 jit_solution(7763856593935259037)
XLA Ops:
  7.2 0.9 copy.25
  8.4 0.7 broadcast_multiply_fusion
  9.1 0.6 reduce-window.6
  10.3 1.4 scatter_custom_fusion
  11.7 1.0 concatenate.9
  12.7 2.8 %gather_fusion = bf16[384,1280]{1,0:T(8,128)(2,1)} fusion(bf16[129,1280]{1,0:T(8,128)(2,1)S(1)} %concatenate.9, s32[1024]{0:T(1024)S(1)} %get-tuple-element.26), kind=kCustom, calls=%fused_computation | custom fusion | bytes 1967616 | tf_op jit(solution)/shard_map/gather | solution.py:47
  15.5 6.3 %all-to-all-start = ((bf16[8,48,1280]{2,1,0:T(8,128)(2,1)}), bf16[8,48,1280]{2,1,0:T(8,128)(2,1)S(1)}, u32[]{:S(2)}, u32[]{:S(2)}) async-start(bf16[8,48,1280]{2,1,0:T(8,128)(2,1)} %bitcast.4), calls=%async_computation | async-start | bytes 1966080 | tf_op jit(solution)/shard_map/all_to_all | solution.py:53
  21.8 1.0 concatenate.10
  22.8 2.8 %gather_fusion.1 = bf16[384,1280]{1,0:T(8,128)(2,1)} fusion(bf16[129,1280]{1,0:T(8,128)(2,1)S(1)} %concatenate.10, s32[1024]{0:T(1024)S(1)} %get-tuple-element.26), kind=kCustom, calls=%fused_computation.1 | custom fusion | bytes 1967616 | tf_op jit(solution)/shard_map/gather | solution.py:48
  25.6 21.4 %all-to-all-done = bf16[8,48,1280]{2,1,0:T(8,128)(2,1)S(1)} async-done(((bf16[8,48,1280]{2,1,0:T(8,128)(2,1)}), bf16[8,48,1280]{2,1,0:T(8,128)(2,1)S(1)}, u32[]{:S(2)}, u32[]{:S(2)}) %all-to-all-start) | async-done | bytes 983072 | tf_op jit(solution)/shard_map/all_to_all | solution.py:53
  47.0 0.9 copy-done.3
  47.9 3.6 %all-to-all-start.1 = ((bf16[8,48,1280]{2,1,0:T(8,128)(2,1)}), bf16[8,48,1280]{2,1,0:T(8,128)(2,1)S(1)}, u32[]{:S(2)}, u32[]{:S(2)}) async-start(bf16[8,48,1280]{2,1,0:T(8,128)(2,1)} %bitcast.107), calls=%async_computation.1 | async-start | bytes 1966080 | tf_op jit(solution)/shard_map/all_to_all | solution.py:60
  51.6 2.9 %fusion.25 = bf16[384,1,768]{2,0,1:T(8,128)(2,1)S(1)} fusion(bf16[384,1280]{1,0:T(8,128)(2,1)} %bitcast.109, bf16[1,1280,768]{2,1,0:T(8,128)(2,1)} %param.12), kind=kOutput, calls=%fused_computation.29 | convolution fusion | flops 755269632 | bytes 3538944 | tf_op jit(solution)/shard_map/dot_general | solution.py:80
  54.4 1.7 fusion.28
  56.2 20.4 %all-to-all-done.1 = bf16[8,48,1280]{2,1,0:T(8,128)(2,1)S(1)} async-done(((bf16[8,48,1280]{2,1,0:T(8,128)(2,1)}), bf16[8,48,1280]{2,1,0:T(8,128)(2,1)S(1)}, u32[]{:S(2)}, u32[]{:S(2)}) %all-to-all-start.1) | async-done | bytes 983072 | tf_op jit(solution)/shard_map/all_to_all | solution.py:60
  76.6 2.9 %fusion.22 = bf16[384,1,768]{2,0,1:T(8,128)(2,1)S(1)} fusion(bf16[384,1280]{1,0:T(8,128)(2,1)S(1)} %bitcast.106, bf16[1,768,1280]{2,1,0:T(8,128)(2,1)} %param.13), kind=kOutput, calls=%fused_computation.28 | convolution fusion | flops 755269632 | bytes 3538944 | tf_op jit(solution)/shard_map/dot_general | solution.py:8
  79.5 1.4 pad_maximum_fusion
  80.9 5.2 %copy.32 = bf16[384,3,768]{0,1,2:T(4,128)(2,1)} copy(bf16[384,3,768]{2,0,1:T(8,128)(2,1)} %pad_maximum_fusion) | data formatting | bytes 3538944
  86.1 3.2 %copy.34 = bf16[96,8,3,384]{3,1,2,0:T(8,128)(2,1)} copy(bf16[96,8,3,384]{3,2,1,0:T(4,128)(2,1)} %bitcast.104) | data formatting | bytes 3538944
  89.7 2.8 %gather_fusion.2 = bf16[384]{0:T(512)(128)(2,1)S(1)} fusion(bf16[257]{0:T(512)(128)(2,1)S(1)} %pad_maximum_fusion.2, s32[1024]{0:T(1024)S(1)} %get-tuple-element.25), kind=kCustom, calls=%fused_computation.2 | custom fusion | bytes 3072 | tf_op jit(solution)/shard_map/gather | solution.py:49
  92.6 7.9 %all_to_all.31 = bf16[8,1,48]{2,1,0:T(2,128)(2,1)S(1)} all-to-all(bf16[8,1,48]{2,1,0:T(2,128)(2,1)S(1)} %all_to_all.25), channel_id=1, replica_groups=mesh['expert'=4,'dp'=8] {'dp'}, dimensions={0} | all-to-all | bytes 1536 | tf_op jit(solution)/shard_map/all_to_all | solution.py:67
  100.6 20.2 %reduce-scatter.4.cloned.1.call-done = bf16[192,1152]{1,0:T(8,128)(2,1)} async-done(((bf16[768,1152]{1,0:T(8,128)(2,1)}), bf16[192,1152]{1,0:T(8,128)(2,1)}) %reduce-scatter.4.cloned.1.call-update) | async-done | bytes 442384
  120.9 1.4 reshape.204
  122.3 1.3 copy.33
  123.6 1.2 convert_element_type.95
  125.0 1.0 pad_maximum_fusion.1
  125.9 2.1 copy.29
  128.3 0.7 convert_element_type.121
  128.9 4.6 %all-to-all-start.4 = ((bf16[8,1,48]{2,1,0:T(2,128)(2,1)}), bf16[8,1,48]{2,1,0:T(2,128)(2,1)S(1)}, u32[]{:S(2)}, u32[]{:S(2)}) async-start(bf16[8,1,48]{2,1,0:T(2,128)(2,1)} %convert_element_type.121), calls=%async_computation.4 | async-start | bytes 8192 | tf_op jit(solution)/shard_map/all_to_all | solution.py:111
  133.5 27.2 %all-gather.2.cloned.1.call-done = bf16[384,3,768]{0,2,1:T(8,128)(2,1)} async-done(((bf16[384,3,192]{0,2,1:T(8,128)(2,1)}), bf16[384,3,768]{0,2,1:T(8,128)(2,1)}) %all-gather.2.cloned.1.call-update) | async-done | bytes 1769488 | tf_op jit(solution)/shard_map/all_gather | solution.py:92
  160.8 2.2 %fusion.9 = f32[384,1280]{1,0:T(8,128)S(1)} fusion(bf16[1,1280,768]{2,1,0:T(8,128)(2,1)S(1)} %copy-done, bf16[384,3,768]{0,2,1:T(8,128)(2,1)} %all-gather.2.cloned.1.call-done), kind=kOutput, calls=%fused_computation.19 | convolution fusion | flops 754974720 | bytes 4521984 | tf_op jit(solution)/shard_map/dot_general | solution.py:8
  163.0 3.1 %fusion.3 = bf16[384,1280]{1,0:T(8,128)(2,1)} fusion(f32[384,1280]{1,0:T(8,128)S(1)} %fusion.9, bf16[1,1280,768]{2,1,0:T(8,128)(2,1)S(1)} %copy-done.9, bf16[384,3,768]{0,2,1:T(8,128)(2,1)} %all-gather.2.cloned.1.call-done), kind=kOutput, calls=%fused_computation.13 | convolution fusion | flops 755957760 | bytes 5505024 | tf_op jit(solution)/shard_map/dot_general | solution.py:8
  166.1 4.7 %all-to-all-start.3 = ((bf16[8,48,1280]{2,1,0:T(8,128)(2,1)}), bf16[8,48,1280]{2,1,0:T(8,128)(2,1)}, u32[]{:S(2)}, u32[]{:S(2)}) async-start(bf16[8,48,1280]{2,1,0:T(8,128)(2,1)} %bitcast.113), calls=%async_computation.3 | async-start | bytes 1966080 | tf_op jit(solution)/shard_map/all_to_all | solution.py:104
  170.9 1.9 gather_fusion.4
  173.0 1.5 collective-permute-start
  174.5 3.0 %collective-permute-done = f32[128,2]{1,0:T(8,128)S(1)} collective-permute-done((f32[128,2]{1,0:T(8,128)S(1)}, f32[128,2]{1,0:T(8,128)S(1)}, u32[]{:S(2)}, u32[]{:S(2)}) %collective-permute-start) | collective-permute-done | bytes 1056 | tf_op jit(solution)/shard_map/ppermute | solution.py:126
  177.6 1.5 collective-permute-start.1
  179.1 1.2 multiply_convert_fusion
  180.3 1.6 collective-permute-done.1
  181.9 0.6 copy.31
  182.6 4.0 %fusion = bf16[1,1280,768]{2,1,0:T(8,128)(2,1)} fusion(bf16[384,1280]{1,0:T(8,128)(2,1)} %bitcast.110, bf16[384,3,768]{0,2,1:T(8,128)(2,1)} %all-gather.2.cloned.1.call-done), kind=kOutput, calls=%fused_computation.10 | convolution fusion | flops 755957760 | bytes 3538944 | tf_op jit(solution)/shard_map/dot_general | solution.py:14
  186.6 2.5 %fusion.1 = bf16[1,1280,768]{2,1,0:T(8,128)(2,1)} fusion(bf16[384,1280]{1,0:T(8,128)(2,1)S(1)} %bitcast.112, bf16[384,3,768]{0,2,1:T(8,128)(2,1)S(1)} %copy-done.10), kind=kOutput, calls=%fused_computation.11 | convolution fusion | flops 755957760 | bytes 3538944 | tf_op jit(solution)/shard_map/dot_general | solution.py:14
  189.1 2.4 %fusion.2 = bf16[1,768,1280]{2,1,0:T(8,128)(2,1)} fusion(bf16[384,1280]{1,0:T(8,128)(2,1)S(1)} %bitcast.114, bf16[384,3,768]{0,2,1:T(8,128)(2,1)S(1)} %copy-done.10), kind=kOutput, calls=%fused_computation.12 | convolution fusion | flops 755957760 | bytes 3538944 | tf_op jit(solution)/shard_map/dot_general | solution.py:14
  191.5 4.6 %all-to-all-done.3 = bf16[8,48,1280]{2,1,0:T(8,128)(2,1)} async-done(((bf16[8,48,1280]{2,1,0:T(8,128)(2,1)}), bf16[8,48,1280]{2,1,0:T(8,128)(2,1)}, u32[]{:S(2)}, u32[]{:S(2)}) %all-to-all-start.3) | async-done | bytes 983072 | tf_op jit(solution)/shard_map/all_to_all | solution.py:104
  196.1 2.6 %bitcast_convert_fusion = f32[384,1280]{1,0:T(8,128)} fusion(bf16[8,48,1280]{2,1,0:T(8,128)(2,1)} %all-to-all-done.3), kind=kLoop, calls=%fused_computation.31 | loop fusion | flops 491520 | bytes 2949120 | tf_op jit(solution)/shard_map/reshape | solution.py:119
  198.7 3.3 %gather_fusion.3 = f32[256,1280]{1,0:T(8,128)S(1)} fusion(f32[384,1280]{1,0:T(8,128)} %bitcast_convert_fusion, s32[1024]{0:T(1024)S(1)} %pad_clamp_fusion), kind=kCustom, calls=%fused_computation.3 | custom fusion | bytes 2622464 | tf_op jit(solution)/shard_map/gather | solution.py:119
  202.1 1.8 reshape.145
  203.9 3.6 %reduce_sum.31 = bf16[128,1280]{1,0:T(8,128)(2,1)} reduce(f32[128,2,1280]{2,1,0:T(2,128)} %reshape.145, f32[]{:T(128)} %constant.40.clone.1), dimensions={1}, to_apply=%region_5.6 | reduce | flops 163840 | bytes 1638404 | tf_op jit(solution)/shard_map/reduce_sum | solution.py:122
  (54 shorter events, 2.3 us)
Async XLA Ops:
  7.2 47.3 %copy-start = (bf16[1,1280,768]{2,1,0:T(8,128)(2,1)S(1)}, bf16[1,1280,768]{2,1,0:T(8,128)(2,1)}, u32[]{:S(2)}) copy-start(bf16[1,1280,768]{2,1,0:T(8,128)(2,1)} %param.11) | copy-start | bytes 5898244
  15.5 31.5 %all-to-all-start = ((bf16[8,48,1280]{2,1,0:T(8,128)(2,1)}), bf16[8,48,1280]{2,1,0:T(8,128)(2,1)S(1)}, u32[]{:S(2)}, u32[]{:S(2)}) async-start(bf16[8,48,1280]{2,1,0:T(8,128)(2,1)} %bitcast.4), calls=%async_computation | async-start | bytes 1966080 | tf_op jit(solution)/shard_map/all_to_all | solution.py:53
  47.0 0.9 copy-start.3
  47.9 28.7 %all-to-all-start.1 = ((bf16[8,48,1280]{2,1,0:T(8,128)(2,1)}), bf16[8,48,1280]{2,1,0:T(8,128)(2,1)S(1)}, u32[]{:S(2)}, u32[]{:S(2)}) async-start(bf16[8,48,1280]{2,1,0:T(8,128)(2,1)} %bitcast.107), calls=%async_computation.1 | async-start | bytes 1966080 | tf_op jit(solution)/shard_map/all_to_all | solution.py:60
  51.5 69.4 %reduce-scatter.4.cloned.1.call-start = ((), (), s32[]{:S(2)}) async-start(), calls=%async_computation.7 | async-start | bytes 2211840
  51.5 2.9 %copy-start.4 = (bf16[8,48,1280]{2,1,0:T(8,128)(2,1)S(1)}, bf16[8,48,1280]{2,1,0:T(8,128)(2,1)}, u32[]{:S(2)}) copy-start(bf16[8,48,1280]{2,1,0:T(8,128)(2,1)} %copy-done.3) | copy-start | bytes 2949124
  76.6 2.9 %copy-start.1 = (bf16[8,48,1280]{2,1,0:T(8,128)(2,1)}, bf16[8,48,1280]{2,1,0:T(8,128)(2,1)S(1)}, u32[]{:S(2)}) copy-start(bf16[8,48,1280]{2,1,0:T(8,128)(2,1)S(1)} %all-to-all-done.1) | copy-start | bytes 2949124
  76.6 2.9 %copy-start.7 = (bf16[384,1,768]{2,0,1:T(8,128)(2,1)S(1)}, bf16[384,1,768]{2,0,1:T(8,128)(2,1)}, u32[]{:S(2)}) copy-start(bf16[384,1,768]{2,0,1:T(8,128)(2,1)} %fusion.28) | copy-start | bytes 1769476
  86.1 3.3 %copy-start.8 = (bf16[128,2]{0,1:T(2,128)(2,1)S(1)}, bf16[128,2]{0,1:T(2,128)(2,1)}, u32[]{:S(2)}) copy-start(bf16[128,2]{0,1:T(2,128)(2,1)} %param.9) | copy-start | bytes 1540
  89.3 71.4 %all-gather.2.cloned.1.call-start = ((), (), s32[]{:S(2)}) async-start(), calls=%async_computation.6 | async-start | bytes 2211840 | tf_op jit(solution)/shard_map/all_gather | solution.py:92
  128.9 37.1 %all-to-all-start.4 = ((bf16[8,1,48]{2,1,0:T(2,128)(2,1)}), bf16[8,1,48]{2,1,0:T(2,128)(2,1)S(1)}, u32[]{:S(2)}, u32[]{:S(2)}) async-start(bf16[8,1,48]{2,1,0:T(2,128)(2,1)} %convert_element_type.121), calls=%async_computation.4 | async-start | bytes 8192 | tf_op jit(solution)/shard_map/all_to_all | solution.py:111
  160.8 2.2 %copy-start.9 = (bf16[1,1280,768]{2,1,0:T(8,128)(2,1)S(1)}, bf16[1,1280,768]{2,1,0:T(8,128)(2,1)}, u32[]{:S(2)}) copy-start(bf16[1,1280,768]{2,1,0:T(8,128)(2,1)} %param.12) | copy-start | bytes 5898244
  166.1 13.1 %copy-start.2 = (bf16[8,48,1280]{2,1,0:T(8,128)(2,1)S(1)}, bf16[8,48,1280]{2,1,0:T(8,128)(2,1)}, u32[]{:S(2)}) copy-start(bf16[8,48,1280]{2,1,0:T(8,128)(2,1)} %copy-done.1) | copy-start | bytes 2949124
  166.1 30.0 %all-to-all-start.3 = ((bf16[8,48,1280]{2,1,0:T(8,128)(2,1)}), bf16[8,48,1280]{2,1,0:T(8,128)(2,1)}, u32[]{:S(2)}, u32[]{:S(2)}) async-start(bf16[8,48,1280]{2,1,0:T(8,128)(2,1)} %bitcast.113), calls=%async_computation.3 | async-start | bytes 1966080 | tf_op jit(solution)/shard_map/all_to_all | solution.py:104
  173.0 4.6 %collective-permute-start = (f32[128,2]{1,0:T(8,128)S(1)}, f32[128,2]{1,0:T(8,128)S(1)}, u32[]{:S(2)}, u32[]{:S(2)}) collective-permute-start(f32[128,2]{1,0:T(8,128)S(1)} %reshape.146), channel_id=1, source_target_pairs={{0,8},{8,0},{16,24},{24,16},{1,9},{9,1},{17,25},{25,17},{2,10},{10... | collective-permute-start | bytes 3080 | tf_op jit(solution)/shard_map/ppermute | solution.py:126
  177.6 4.3 %collective-permute-start.1 = (f32[128,2]{1,0:T(8,128)S(1)}, f32[128,2]{1,0:T(8,128)S(1)}, u32[]{:S(2)}, u32[]{:S(2)}) collective-permute-start(f32[128,2]{1,0:T(8,128)S(1)} %add.69), channel_id=1, source_target_pairs={{0,16},{8,24},{16,0},{24,8},{1,17},{9,25},{17,1},{25,9},{2,18},{10... | collective-permute-start | bytes 3080 | tf_op jit(solution)/shard_map/ppermute | solution.py:126
  180.3 6.3 %copy-start.5 = (bf16[8,48,1280]{2,1,0:T(8,128)(2,1)S(1)}, bf16[8,48,1280]{2,1,0:T(8,128)(2,1)}, u32[]{:S(2)}) copy-start(bf16[8,48,1280]{2,1,0:T(8,128)(2,1)} %copy-done.3) | copy-start | bytes 2949124
  182.6 4.0 %copy-start.10 = (bf16[384,3,768]{0,2,1:T(8,128)(2,1)S(1)}, bf16[384,3,768]{0,2,1:T(8,128)(2,1)}, u32[]{:S(2)}) copy-start(bf16[384,3,768]{0,2,1:T(8,128)(2,1)} %all-gather.2.cloned.1.call-done) | copy-start | bytes 5308420
  186.6 2.5 %copy-start.6 = (bf16[8,48,1280]{2,1,0:T(8,128)(2,1)S(1)}, bf16[8,48,1280]{2,1,0:T(8,128)(2,1)}, u32[]{:S(2)}) copy-start(bf16[8,48,1280]{2,1,0:T(8,128)(2,1)} %multiply_convert_fusion) | copy-start | bytes 2949124
Sparse Core Ops, SparseCore 0:
  89.5 31.3 reduce-scatter.3
  128.2 32.5 all-gather.1
